TPU v7x, 32 devices: a whole 2x2x4 slice. The times are simulated.
32 devices in a mesh: loss: 4 (over x, core), tower: 4 (over z), pipe: 2 (over y).
Axes of the slice: x: 2, y: 2, z: 4, core: 2. Of those that a mesh axis runs over, the one named last changes fastest.
Arguments:
- image_feats: bfloat16 [4, 2, 24, 1536], P('loss', 'pipe', None, 'tower'), may hold values from -6 to 6
- text_tokens: bfloat16 [4, 2, 24, 64, 1152], P('loss', 'pipe', None, None, 'tower'), may hold values from -6 to 6
- lengths: int32 [4, 2, 24], P('loss', 'pipe'), may hold values from 1 to 64, as said below
- w_image: bfloat16 [1536, 1536], P('tower'), may hold values from -0.15625 to 0.15625
- w_text: bfloat16 [1152, 1536], P('tower'), may hold values from -0.1875 to 0.1875
- logit_scale: float32 [1], replicated, may hold values from 24 to 48
- logit_bias: float32 [1], replicated, may hold values from -4 to -2
Outputs:
- image_grad: float32 [4, 2, 24, 1536], P('loss', 'pipe', 'tower')
- text_grad: float32 [4, 2, 24, 1536], P('loss', 'pipe', 'tower')
Inputs may be any that keep to these rules, and one draw needn't show every extreme that they name: `lengths`: in every group of 24 captions one caption has 64 tokens and one has a single token.
All inputs are finite; a program needn't handle non-finite values.
Results may differ from a plain program's by a relative error of at most 0.0036.
The roundings to bfloat16 on the way count: a program that leaves them out, or rounds other values in their place, can miss the bound.
Values may be sent and summed in bfloat16 or wider, within the bound.
A program may use at most 64 MiB of HBM per device.

v0:
```python
import jax
import jax.numpy as jnp
from jax import lax
from jax.sharding import PartitionSpec as P


def normalize(raw):
    return raw * lax.rsqrt(jnp.sum(raw * raw, axis=-1, keepdims=True) + 1e-06)


def pair_terms(image_unit, texts, image_ids, text_ids, scale, shift):
    scores = jnp.dot(image_unit, texts.T, preferred_element_type=jnp.float32)
    match = (image_ids[:, None] == text_ids[None, :]).astype(jnp.float32)
    return (jax.nn.sigmoid(scale * scores + shift) - match).astype(jnp.bfloat16)


def per_device(image_feats, text_tokens, lengths, w_image, w_text, logit_scale, logit_bias):
    group = image_feats.shape[2]
    emb = w_image.shape[1]
    images = image_feats.reshape(group, image_feats.shape[3])
    words = text_tokens.reshape(group, text_tokens.shape[3], text_tokens.shape[4])
    counts = lengths.reshape(group)
    places = lax.broadcasted_iota(jnp.int32, (group, words.shape[1]), 1)
    keep = (places < counts[:, None]).astype(jnp.bfloat16)
    summed = jnp.einsum("bl,bld->bd", keep, words, preferred_element_type=jnp.float32)
    pooled = (summed / counts.astype(jnp.float32)[:, None]).astype(jnp.bfloat16)
    image_raw = lax.psum(jnp.dot(images, w_image, preferred_element_type=jnp.float32), "tower")
    towers = lax.axis_size("tower")
    sub = group // towers
    text_raw = lax.psum_scatter(
        jnp.dot(pooled, w_text, preferred_element_type=jnp.float32),
        "tower",
        scatter_dimension=0,
        tiled=True,
    )
    image_unit = normalize(image_raw).astype(jnp.bfloat16)
    text_unit = normalize(text_raw).astype(jnp.bfloat16)
    scale = logit_scale[0]
    shift = logit_bias[0]
    loss_at = lax.axis_index("loss")
    pipe_at = lax.axis_index("pipe")
    tower_at = lax.axis_index("tower")
    pipes = lax.axis_size("pipe")
    image_ids = (loss_at * pipes + pipe_at) * group + lax.iota(jnp.int32, group)
    texts = lax.all_gather(text_unit, ("loss", "pipe"), axis=0, tiled=True)
    spots = lax.iota(jnp.int32, texts.shape[0])
    text_ids = spots // sub * group + tower_at * sub + spots % sub
    grads = pair_terms(image_unit, texts, image_ids, text_ids, scale, shift)
    image_term = scale * jnp.dot(grads, texts, preferred_element_type=jnp.float32)
    text_grad = lax.psum_scatter(
        scale
        * lax.dot_general(
            grads, image_unit, (((0,), (0,)), ((), ())), preferred_element_type=jnp.float32
        ),
        ("loss", "pipe"),
        scatter_dimension=0,
        tiled=True,
    )
    image_grad = lax.psum_scatter(image_term, "tower", scatter_dimension=0, tiled=True)
    return (image_grad.reshape(1, 1, sub, emb), text_grad.reshape(1, 1, sub, emb))


def solution(mesh):
    return jax.shard_map(
        per_device,
        mesh=mesh,
        in_specs=(
            P("loss", "pipe", None, "tower"),
            P("loss", "pipe", None, None, "tower"),
            P("loss", "pipe", None),
            P("tower", None),
            P("tower", None),
            P(),
            P(),
        ),
        out_specs=(P("loss", "pipe", "tower", None), P("loss", "pipe", "tower", None)),
        check_vma=False,
    )
```

profile of v0, /device:TPU:1, one launch (start us, length us, event | category | flops | bytes accessed | tf_op | source)
XLA Modules:
  0.0 116.7 jit_solution(13100694398209393492)
XLA Ops:
  7.2 0.8 bitcast_convert_fusion
  8.0 0.7 fusion.20
  8.8 1.6 %fusion.3 = f32[24,1,288]{2,1,0:T(1,128)S(1)} fusion(bf16[1,1,24,64,288]{4,3,2,1,0:T(8,128)(2,1)} %param.8, pred[24,64,1]{1,0,2:T(8,128)(4,1)S(1)} %fusion.20), kind=kOutput, calls=%fused_computation.2 | convolution fusion | flops 884736 | bytes 913920 | tf_op jit(solution)/shard_map/bl,bld->bd/dot_general | solution.py:25
  10.3 0.3 fusion.15
  10.7 12.8 %fusion = f32[8,1536]{1,0:T(8,128)S(1)} fusion(f32[24,1536]{1,0:T(8,128)S(1)} %fusion.15), kind=kCustom, calls=%all-reduce-scatter | all-reduce-scatter fusion | flops 49153 | bytes 197120
  23.5 2.0 %collective-permute-start = (f32[6,1536]{1,0:T(8,128)S(1)}, f32[6,1536]{1,0:T(8,128)S(1)}, u32[]{:S(2)}, u32[]{:S(2)}) collective-permute-start(f32[6,1536]{1,0:T(8,128)S(1)} %slice), channel_id=1, source_target_pairs={{0,2},{2,4},{4,6},{1,3},{3,5},{5,7},{8,10},{10,12},{12,14},{9,11},... | collective-permute-start | bytes 110600
  25.5 0.9 fusion.17
  27.8 0.6 dynamic-slice.8
  28.4 0.7 dynamic-slice.16
  30.8 19.7 %all-gather = bf16[8,6,1536]{2,1,0:T(8,128)(2,1)S(1)} all-gather(bf16[1,6,1536]{2,1,0:T(8,128)(2,1)S(1)} %fusion.14), channel_id=1, replica_groups=mesh['loss'=4,'tower'=4,'pipe'=2] {'loss','pipe'}, dimensions={0}, use_global_device_ids=true | all-gather | bytes 165888 | tf_op jit(solution)/shard_map/all_gather | solution.py:45
  50.5 10.2 %all-reduce.8.cloned.1.call-done = f32[24,1536]{1,0:T(8,128)} async-done(((f32[24,1536]{1,0:T(8,128)}), f32[24,1536]{1,0:T(8,128)}) %all-reduce.8.cloned.1.call-update) | async-done | bytes 147472 | tf_op jit(solution)/shard_map/psum | solution.py:27
  60.7 1.0 multiply_reduce_fusion
  61.7 1.2 fusion.11
  62.9 0.1 convolution_multiply_fusion.1
  63.0 12.3 %fusion.1 = f32[8,1536]{1,0:T(8,128)S(1)} fusion(f32[24,1536]{1,0:T(8,128)S(1)} %convolution_multiply_fusion.1), kind=kCustom, calls=%all-reduce-scatter.1 | all-reduce-scatter fusion | flops 49153 | bytes 197120
  75.3 1.6 %collective-permute-start.1 = (f32[6,1536]{1,0:T(8,128)S(1)}, f32[6,1536]{1,0:T(8,128)S(1)}, u32[]{:S(2)}, u32[]{:S(2)}) collective-permute-start(f32[6,1536]{1,0:T(8,128)S(1)} %slice.1), channel_id=1, source_target_pairs={{0,2},{2,4},{4,6},{1,3},{3,5},{5,7},{8,10},{10,12},{12,14},{9,11},... | collective-permute-start | bytes 110600
  76.9 1.2 convolution_multiply_fusion
  78.0 23.2 %fusion.2 = f32[8,1536]{1,0:T(8,128)S(1)} fusion(f32[48,1536]{1,0:T(8,128)S(1)} %convolution_multiply_fusion), kind=kCustom, calls=%all-reduce-scatter.2 | all-reduce-scatter fusion | flops 98305 | bytes 344576
  101.2 1.9 %collective-permute-start.2 = (f32[8,1536]{1,0:T(8,128)S(1)}, f32[8,1536]{1,0:T(8,128)S(1)}, u32[]{:S(2)}, u32[]{:S(2)}) collective-permute-start(f32[8,1536]{1,0:T(8,128)S(1)} %fusion.2), channel_id=1, source_target_pairs={{0,1},{1,8},{8,9},{9,16},{16,17},{17,24},{24,25},{2,3},{3,10},{10,... | collective-permute-start | bytes 147464
  103.2 4.6 %collective-permute-start.3 = (f32[6,1536]{1,0:T(8,128)S(1)}, f32[6,1536]{1,0:T(8,128)S(1)}, u32[]{:S(2)}, u32[]{:S(2)}) collective-permute-start(f32[6,1536]{1,0:T(8,128)S(1)} %slice.2), channel_id=1, source_target_pairs={{0,8},{1,9},{8,16},{9,17},{16,24},{17,25},{2,10},{3,11},{10,18},{1... | collective-permute-start | bytes 110600
  107.9 0.7 copy.13
  108.6 0.3 collective-permute-done.3
  108.9 0.2 concatenate.2
  109.2 0.7 copy.14
  (29 shorter events, 0.7 us)
Async XLA Ops:
  7.2 18.3 %copy-start = (bf16[384,1536]{1,0:T(8,128)(2,1)S(1)}, bf16[384,1536]{1,0:T(8,128)(2,1)}, u32[]{:S(2)}) copy-start(bf16[384,1536]{1,0:T(8,128)(2,1)} %param.10) | copy-start | bytes 3538948
  7.2 3.2 %copy-start.1 = (bf16[288,1536]{1,0:T(8,128)(2,1)S(1)}, bf16[288,1536]{1,0:T(8,128)(2,1)}, u32[]{:S(2)}) copy-start(bf16[288,1536]{1,0:T(8,128)(2,1)} %param.11) | copy-start | bytes 2654212
  7.2 53.5 %all-reduce.8.cloned.1.call-start = ((), (), s32[]{:S(2)}) async-start(), calls=%async_computation | async-start | bytes 294912 | tf_op jit(solution)/shard_map/psum | solution.py:27
  8.8 16.8 %copy-start.2 = (bf16[1,1,24,384]{3,2,1,0:T(8,128)(2,1)S(1)}, bf16[1,1,24,384]{3,2,1,0:T(8,128)(2,1)}, u32[]{:S(2)}) copy-start(bf16[1,1,24,384]{3,2,1,0:T(8,128)(2,1)} %param.7) | copy-start | bytes 55300
  10.6 17.2 %copy-start.4 = (u32[32]{0:T(128)S(1)}, u32[32]{0:T(128)}, u32[]{:S(2)}) copy-start(u32[32]{0:T(128)} %constant.48) | copy-start | bytes 388
  10.6 17.8 %copy-start.3 = (u32[32]{0:T(128)S(1)}, u32[32]{0:T(128)}, u32[]{:S(2)}) copy-start(u32[32]{0:T(128)} %constant.56) | copy-start | bytes 388
  23.5 6.9 %collective-permute-start = (f32[6,1536]{1,0:T(8,128)S(1)}, f32[6,1536]{1,0:T(8,128)S(1)}, u32[]{:S(2)}, u32[]{:S(2)}) collective-permute-start(f32[6,1536]{1,0:T(8,128)S(1)} %slice), channel_id=1, source_target_pairs={{0,2},{2,4},{4,6},{1,3},{3,5},{5,7},{8,10},{10,12},{12,14},{9,11},... | collective-permute-start | bytes 110600
  75.3 32.4 %collective-permute-start.1 = (f32[6,1536]{1,0:T(8,128)S(1)}, f32[6,1536]{1,0:T(8,128)S(1)}, u32[]{:S(2)}, u32[]{:S(2)}) collective-permute-start(f32[6,1536]{1,0:T(8,128)S(1)} %slice.1), channel_id=1, source_target_pairs={{0,2},{2,4},{4,6},{1,3},{3,5},{5,7},{8,10},{10,12},{12,14},{9,11},... | collective-permute-start | bytes 110600
  101.2 7.7 %collective-permute-start.2 = (f32[8,1536]{1,0:T(8,128)S(1)}, f32[8,1536]{1,0:T(8,128)S(1)}, u32[]{:S(2)}, u32[]{:S(2)}) collective-permute-start(f32[8,1536]{1,0:T(8,128)S(1)} %fusion.2), channel_id=1, source_target_pairs={{0,1},{1,8},{8,9},{9,16},{16,17},{17,24},{24,25},{2,3},{3,10},{10,... | collective-permute-start | bytes 147464
  103.2 5.8 %collective-permute-start.3 = (f32[6,1536]{1,0:T(8,128)S(1)}, f32[6,1536]{1,0:T(8,128)S(1)}, u32[]{:S(2)}, u32[]{:S(2)}) collective-permute-start(f32[6,1536]{1,0:T(8,128)S(1)} %slice.2), channel_id=1, source_target_pairs={{0,8},{1,9},{8,16},{9,17},{16,24},{17,25},{2,10},{3,11},{10,18},{1... | collective-permute-start | bytes 110600
Sparse Core Ops, SparseCore 0:
  26.6 34.0 all-reduce.7
where the time goes:
time: 117 us
  blocking collectives  67.9 us (58%)
  between operations  16.9 us (14%)
  waiting for transfers between devices  10.5 us (9%)
  starting transfers between devices  10.1 us (9%)
  matrix products  5.25 us (4%)
  local copies, waits for them, and re-layouts  3.18 us (3%)
  other arithmetic  2.8 us (2%)
    unnamed x3, blocking collectives  48.2 us
    all_gather x1, blocking collectives, per_device(): texts = lax.all_gather(text_unit, ('loss', 'pipe'), axis=0, tiled=True)  19.7 us
    psum x1, waiting for transfers between devices, per_device(): lax.psum(jnp.dot(images, w_image, preferred_element_type=jnp.float32), 't...  10.2 us
    unnamed x4, starting transfers between devices  10.1 us
    unnamed x21, local copies, waits for them, and re-layouts  3.15 us
  transfers between devices with their start and end apart: 5, of which 2 were waited for; matrix products, arithmetic and copies ran while one was open for 24% of the time, Pallas kernels for 0%

commit v1 on v0

--- a/solution.py
+++ b/solution.py
@@ -24,7 +24,9 @@
     keep = (places < counts[:, None]).astype(jnp.bfloat16)
     summed = jnp.einsum("bl,bld->bd", keep, words, preferred_element_type=jnp.float32)
     pooled = (summed / counts.astype(jnp.float32)[:, None]).astype(jnp.bfloat16)
-    image_raw = lax.psum(jnp.dot(images, w_image, preferred_element_type=jnp.float32), "tower")
+    own = jnp.dot(images, w_image, preferred_element_type=jnp.float32)
+    parts = lax.all_gather(own, "tower")
+    image_raw = jnp.sum(parts, axis=0)
     towers = lax.axis_size("tower")
     sub = group // towers
     text_raw = lax.psum_scatter(

time: 117 us -> 101 us (0.86)
  between operations: 16.9 us -> 3.39 us
  blocking collectives: 67.9 us -> 78.6 us
  waiting for transfers between devices: 10.5 us -> 0.34 us
  matrix products: 5.25 us -> 2.76 us
    all_gather x0 -> x1, blocking collectives: none -> 13.8 us  [per_device(): parts = lax.all_gather(own, 'tower')]
    psum x1 -> x0, waiting for transfers between devices: 10.2 us -> none  [per_device(): lax.psum(jnp.dot(images, w_image, preferred_element_type=jnp.float32), 't...]
    unnamed x3, blocking collectives: 48.2 us -> 43.7 us
    all_gather x1, blocking collectives: 19.7 us -> 21.1 us  [per_device(): texts = lax.all_gather(text_unit, ('loss', 'pipe'), axis=0, tiled=True)]
  transfers between devices with their start and end apart: 5 -> 4, of which waited for: 2 -> 1; matrix products, arithmetic and copies ran while one was open for 24% -> 23% of each run, Pallas kernels for 0% -> 0%
where the time goes in v1:
time: 101 us; the launch traced here: 100 us
  blocking collectives  78.6 us (78%)
  starting transfers between devices  10 us (10%)
  between operations  3.39 us (3%)
  local copies, waits for them, and re-layouts  3.1 us (3%)
  matrix products  2.76 us (3%)
  other arithmetic  1.93 us (2%)
    unnamed x3, blocking collectives  43.7 us
    all_gather x1, blocking collectives, per_device(): texts = lax.all_gather(text_unit, ('loss', 'pipe'), axis=0, tiled=True)  21.1 us
    all_gather x1, blocking collectives, per_device(): parts = lax.all_gather(own, 'tower')  13.8 us
    unnamed x4, starting transfers between devices  10 us
    unnamed x21, local copies, waits for them, and re-layouts  3.07 us
  transfers between devices with their start and end apart: 4, of which 1 were waited for; matrix products, arithmetic and copies ran while one was open for 23% of the time, Pallas kernels for 0%

profile of v1, /device:TPU:1, one launch (start us, length us, event | category | flops | bytes accessed | tf_op | source)
XLA Modules:
  0.0 100.1 jit_solution(12646328454072607233)
XLA Ops:
  0.7 0.8 bitcast_convert_fusion
  1.5 0.7 fusion.20
  2.2 1.6 %fusion.3 = f32[24,1,288]{2,1,0:T(1,128)S(1)} fusion(bf16[1,1,24,64,288]{4,3,2,1,0:T(8,128)(2,1)} %param.8, pred[24,64,1]{1,0,2:T(8,128)(4,1)S(1)} %fusion.20), kind=kOutput, calls=%fused_computation.2 | convolution fusion | flops 884736 | bytes 913920 | tf_op jit(solution)/shard_map/bl,bld->bd/dot_general | solution.py:25
  3.8 0.3 fusion.15
  4.1 12.7 %fusion = f32[8,1536]{1,0:T(8,128)S(1)} fusion(f32[24,1536]{1,0:T(8,128)S(1)} %fusion.15), kind=kCustom, calls=%all-reduce-scatter | all-reduce-scatter fusion | flops 49153 | bytes 197120
  16.8 2.0 %collective-permute-start = (f32[6,1536]{1,0:T(8,128)S(1)}, f32[6,1536]{1,0:T(8,128)S(1)}, u32[]{:S(2)}, u32[]{:S(2)}) collective-permute-start(f32[6,1536]{1,0:T(8,128)S(1)} %slice), channel_id=1, source_target_pairs={{0,2},{2,4},{4,6},{1,3},{3,5},{5,7},{8,10},{10,12},{12,14},{9,11},... | collective-permute-start | bytes 110600
  18.9 0.3 fusion.17
  19.1 13.8 %all-gather = f32[96,1536]{1,0:T(8,128)S(1)} all-gather(f32[24,1536]{1,0:T(8,128)S(1)} %fusion.17), channel_id=2, replica_groups=mesh['loss'=4,'tower'=4,'pipe'=2] {'tower'}, dimensions={0}, use_global_device_ids=true | all-gather | bytes 737280 | tf_op jit(solution)/shard_map/all_gather | solution.py:28
  34.4 0.6 dynamic-slice.8
  35.0 0.6 dynamic-slice.16
  36.9 0.1 multiply_reduce_fusion.1
  37.1 21.1 %all-gather.1 = bf16[8,6,1536]{2,1,0:T(8,128)(2,1)S(1)} all-gather(bf16[1,6,1536]{2,1,0:T(8,128)(2,1)S(1)} %fusion.14), channel_id=1, replica_groups=mesh['loss'=4,'tower'=4,'pipe'=2] {'loss','pipe'}, dimensions={0}, use_global_device_ids=true | all-gather | bytes 165888 | tf_op jit(solution)/shard_map/all_gather | solution.py:47
  58.3 0.2 fusion.11
  58.6 0.2 convolution_multiply_fusion
  58.8 0.1 convolution_multiply_fusion.1
  59.0 10.6 %fusion.1 = f32[8,1536]{1,0:T(8,128)S(1)} fusion(f32[24,1536]{1,0:T(8,128)S(1)} %convolution_multiply_fusion.1), kind=kCustom, calls=%all-reduce-scatter.1 | all-reduce-scatter fusion | flops 49153 | bytes 197120
  69.6 1.5 %collective-permute-start.1 = (f32[6,1536]{1,0:T(8,128)S(1)}, f32[6,1536]{1,0:T(8,128)S(1)}, u32[]{:S(2)}, u32[]{:S(2)}) collective-permute-start(f32[6,1536]{1,0:T(8,128)S(1)} %slice.1), channel_id=1, source_target_pairs={{0,2},{2,4},{4,6},{1,3},{3,5},{5,7},{8,10},{10,12},{12,14},{9,11},... | collective-permute-start | bytes 110600
  71.1 20.4 %fusion.2 = f32[8,1536]{1,0:T(8,128)S(1)} fusion(f32[48,1536]{1,0:T(8,128)S(1)} %convolution_multiply_fusion), kind=kCustom, calls=%all-reduce-scatter.2 | all-reduce-scatter fusion | flops 98305 | bytes 344576
  91.5 1.9 %collective-permute-start.2 = (f32[8,1536]{1,0:T(8,128)S(1)}, f32[8,1536]{1,0:T(8,128)S(1)}, u32[]{:S(2)}, u32[]{:S(2)}) collective-permute-start(f32[8,1536]{1,0:T(8,128)S(1)} %fusion.2), channel_id=1, source_target_pairs={{0,1},{1,8},{8,9},{9,16},{16,17},{17,24},{24,25},{2,3},{3,10},{10,... | collective-permute-start | bytes 147464
  93.4 4.6 %collective-permute-start.3 = (f32[6,1536]{1,0:T(8,128)S(1)}, f32[6,1536]{1,0:T(8,128)S(1)}, u32[]{:S(2)}, u32[]{:S(2)}) collective-permute-start(f32[6,1536]{1,0:T(8,128)S(1)} %slice.2), channel_id=1, source_target_pairs={{0,8},{1,9},{8,16},{9,17},{16,24},{17,25},{2,10},{3,11},{10,18},{1... | collective-permute-start | bytes 110600
  98.2 0.7 copy.15
  98.9 0.3 collective-permute-done.3
  99.2 0.2 concatenate.2
  99.5 0.7 copy.16
  (28 shorter events, 0.7 us)
Async XLA Ops:
  0.6 18.2 %copy-start = (bf16[384,1536]{1,0:T(8,128)(2,1)S(1)}, bf16[384,1536]{1,0:T(8,128)(2,1)}, u32[]{:S(2)}) copy-start(bf16[384,1536]{1,0:T(8,128)(2,1)} %param.10) | copy-start | bytes 3538948
  0.6 3.1 %copy-start.1 = (bf16[288,1536]{1,0:T(8,128)(2,1)S(1)}, bf16[288,1536]{1,0:T(8,128)(2,1)}, u32[]{:S(2)}) copy-start(bf16[288,1536]{1,0:T(8,128)(2,1)} %param.11) | copy-start | bytes 2654212
  2.2 16.6 %copy-start.2 = (bf16[1,1,24,384]{3,2,1,0:T(8,128)(2,1)S(1)}, bf16[1,1,24,384]{3,2,1,0:T(8,128)(2,1)}, u32[]{:S(2)}) copy-start(bf16[1,1,24,384]{3,2,1,0:T(8,128)(2,1)} %param.7) | copy-start | bytes 55300
  16.8 20.0 %collective-permute-start = (f32[6,1536]{1,0:T(8,128)S(1)}, f32[6,1536]{1,0:T(8,128)S(1)}, u32[]{:S(2)}, u32[]{:S(2)}) collective-permute-start(f32[6,1536]{1,0:T(8,128)S(1)} %slice), channel_id=1, source_target_pairs={{0,2},{2,4},{4,6},{1,3},{3,5},{5,7},{8,10},{10,12},{12,14},{9,11},... | collective-permute-start | bytes 110600
  18.8 15.5 %copy-start.4 = (u32[32]{0:T(128)S(1)}, u32[32]{0:T(128)}, u32[]{:S(2)}) copy-start(u32[32]{0:T(128)} %constant.48) | copy-start | bytes 388
  18.8 16.1 %copy-start.3 = (u32[32]{0:T(128)S(1)}, u32[32]{0:T(128)}, u32[]{:S(2)}) copy-start(u32[32]{0:T(128)} %constant.56) | copy-start | bytes 388
  69.6 28.4 %collective-permute-start.1 = (f32[6,1536]{1,0:T(8,128)S(1)}, f32[6,1536]{1,0:T(8,128)S(1)}, u32[]{:S(2)}, u32[]{:S(2)}) collective-permute-start(f32[6,1536]{1,0:T(8,128)S(1)} %slice.1), channel_id=1, source_target_pairs={{0,2},{2,4},{4,6},{1,3},{3,5},{5,7},{8,10},{10,12},{12,14},{9,11},... | collective-permute-start | bytes 110600
  91.5 7.7 %collective-permute-start.2 = (f32[8,1536]{1,0:T(8,128)S(1)}, f32[8,1536]{1,0:T(8,128)S(1)}, u32[]{:S(2)}, u32[]{:S(2)}) collective-permute-start(f32[8,1536]{1,0:T(8,128)S(1)} %fusion.2), channel_id=1, source_target_pairs={{0,1},{1,8},{8,9},{9,16},{16,17},{17,24},{24,25},{2,3},{3,10},{10,... | collective-permute-start | bytes 147464
  93.4 5.8 %collective-permute-start.3 = (f32[6,1536]{1,0:T(8,128)S(1)}, f32[6,1536]{1,0:T(8,128)S(1)}, u32[]{:S(2)}, u32[]{:S(2)}) collective-permute-start(f32[6,1536]{1,0:T(8,128)S(1)} %slice.2), channel_id=1, source_target_pairs={{0,8},{1,9},{8,16},{9,17},{16,24},{17,25},{2,10},{3,11},{10,18},{1... | collective-permute-start | bytes 110600
